TPU v7x, 32 devices: a whole 2x2x4 slice. The times are simulated.
32 devices in a mesh: row: 8 (over y, x, core), col: 4 (over z).
Axes of the slice: x: 2, y: 2, z: 4, core: 2. Of those that a mesh axis runs over, the one named last changes fastest.
Arguments:
- student_in: bfloat16 [768, 8192], P('col', 'row'), may hold values from -6 to 6
- norm_gain: bfloat16 [8192], P('row'), may hold values from 0.099609375 to 1.8984375
- w_gate: bfloat16 [8192, 28672], P('row', 'col'), may hold values from -0.0625 to 0.0625
- w_up: bfloat16 [8192, 28672], P('row', 'col'), may hold values from -0.0625 to 0.0625
- w_down: bfloat16 [28672, 8192], P('col', 'row'), may hold values from -0.03125 to 0.03125
- teacher: bfloat16 [2, 768, 8192], P(None, 'col', 'row'), may hold values from -6 to 6
- layer_map: int32 [2], replicated, may hold values from 0 to 1, each once
Outputs:
- student_out: bfloat16 [768, 8192], P('col', 'row')
- match_loss: float32 [], replicated
Inputs may be any that keep to these rules, and one draw needn't show every extreme that they name: `layer_map`: a permutation of 0 to 1.
All inputs are finite; a program needn't handle non-finite values.
Results may differ from a plain program's by a relative error of at most 0.014.
Values may be sent and summed in bfloat16 or wider, within the bound.
A program may use at most 192 MiB of HBM per device.

v0:
```python
import jax
import jax.numpy as jnp
from jax import lax
from jax.sharding import PartitionSpec as P

D = 8192


def swiglu(both, width):
    return (jax.nn.silu(both[:, :width]) * both[:, width:]).astype(jnp.bfloat16)


def body(student_in, norm_gain, w_gate, w_up, w_down, teacher, layer_map):
    xf = student_in.astype(jnp.float32)
    squares = lax.psum(jnp.sum(xf * xf, axis=1), "row")
    mean_sq = squares / D
    normed = (
        xf * lax.rsqrt(mean_sq[:, None] + 1e-05) * norm_gain.astype(jnp.float32)[None, :]
    ).astype(jnp.bfloat16)
    all_rows = lax.all_gather(normed, "col", axis=0, tiled=True)
    width = w_gate.shape[1]
    piece = all_rows
    first = jnp.dot(piece, w_gate, preferred_element_type=jnp.float32)
    second = jnp.dot(piece, w_up, preferred_element_type=jnp.float32)
    mine = lax.psum_scatter(
        jnp.concatenate([first, second], axis=1).astype(jnp.bfloat16),
        "row",
        scatter_dimension=0,
        tiled=True,
    ).astype(jnp.float32)
    hidden_all = lax.all_gather(swiglu(mine, width), "row", axis=0, tiled=True)
    piece = hidden_all
    branch = lax.psum_scatter(
        jnp.dot(piece, w_down, preferred_element_type=jnp.float32).astype(jnp.bfloat16),
        "col",
        scatter_dimension=0,
        tiled=True,
    ).astype(jnp.float32)
    student_out = (xf + branch).astype(jnp.bfloat16)
    target = lax.dynamic_index_in_dim(teacher, layer_map[0], 0, keepdims=False).astype(jnp.float32)
    diff = student_out.astype(jnp.float32) - target
    total = lax.psum(jnp.sum(diff * diff), ("row", "col"))
    count_all = student_in.shape[0] * lax.axis_size("col") * D
    return (student_out, total / count_all)


def solution(mesh):
    placed = (
        P("col", "row"),
        P("row"),
        P("row", "col"),
        P("row", "col"),
        P("col", "row"),
        P(None, "col", "row"),
        P(),
    )
    return jax.shard_map(
        body, mesh=mesh, in_specs=placed, out_specs=(P("col", "row"), P()), check_vma=False
    )
```

profile of v0, /device:TPU:0, one launch (start us, length us, event | category | flops | bytes accessed | tf_op | source)
XLA Modules:
  0.0 428.6 jit_solution(13553694904345614874)
XLA Ops:
  7.2 0.0 all-gather.3.cloned.1.call-start
  7.2 1.2 fusion.1
  8.4 15.1 %psum.14 = f32[192]{0:T(256)S(1)} all-reduce(f32[192]{0:T(256)S(1)} %fusion.1), channel_id=1, replica_groups=mesh['row'=8,'col'=4] {'row'}, use_global_device_ids=true, to_apply=%region_1.0 | all-reduce | flops 192 | bytes 1536 | tf_op jit(solution)/shard_map/psum | solution.py:15
  23.5 0.7 convert_element_type.35
  24.2 1.9 fusion.3
  26.1 0.0 all-gather.3.cloned.1.call-update
  26.1 0.0 reduce-scatter.3.cloned.1.call-start
  26.2 36.5 %all-gather.3.cloned.1.call-done = bf16[768,1024]{1,0:T(8,128)(2,1)} async-done(((bf16[192,1024]{1,0:T(8,128)(2,1)}), bf16[768,1024]{1,0:T(8,128)(2,1)}) %all-gather.3.cloned.1.call-update) | async-done | bytes 1572880 | tf_op jit(solution)/shard_map/all_gather | solution.py:20
  62.7 0.0 copy-start.3
  62.7 17.3 %convolution_convert_fusion = bf16[768,7168]{1,0:T(8,128)(2,1)S(1)} fusion(bf16[768,1024]{1,0:T(8,128)(2,1)} %all-gather.3.cloned.1.call-done, bf16[1024,7168]{1,0:T(8,128)(2,1)} %param.10), kind=kOutput, calls=%fused_computation.1 | convolution fusion | flops 11279794176 | bytes 27262976 | tf_op jit(solution)/shard_map/dot_general | solution.py:24
  79.9 0.0 copy-done.3
  80.0 19.0 %convolution_convert_fusion.1 = bf16[768,7168]{1,0:T(8,128)(2,1)} fusion(bf16[768,1024]{1,0:T(8,128)(2,1)S(1)} %copy-done.3, bf16[1024,7168]{1,0:T(8,128)(2,1)} %param.9), kind=kOutput, calls=%fused_computation.2 | convolution fusion | flops 11279794176 | bytes 27262976 | tf_op jit(solution)/shard_map/dot_general | solution.py:23
  98.9 16.5 %pad_maximum_fusion = bf16[768,14336]{1,0:T(8,128)(2,1)} fusion(bf16[768,7168]{1,0:T(8,128)(2,1)S(1)} %convolution_convert_fusion, bf16[768,7168]{1,0:T(8,128)(2,1)} %convolution_convert_fusion.1), kind=kLoop, calls=%fused_computation | loop fusion | flops 44040192 | bytes 44040192 | tf_op jit(solution)/shard_map/concatenate | solution.py:26
  115.4 0.0 reduce-scatter.3.cloned.1.call-update
  115.4 0.0 all-gather.5.cloned.1.call-start
  115.5 140.1 %reduce-scatter.3.cloned.1.call-done = bf16[96,14336]{1,0:T(8,128)(2,1)} async-done(((bf16[768,14336]{1,0:T(8,128)(2,1)}), bf16[96,14336]{1,0:T(8,128)(2,1)}) %reduce-scatter.3.cloned.1.call-update) | async-done | bytes 2752528 | tf_op jit(solution)/shard_map/reduce_scatter | solution.py:25
  255.5 2.3 convert_element_type.37
  257.8 1.8 fusion
  259.6 0.0 all-gather.5.cloned.1.call-update
  259.6 0.0 copy-start.2
  259.6 0.0 copy-start
  259.6 0.0 copy-start.1
  259.6 0.2 reduce-scatter.5.cloned.1.call-start
  259.9 65.2 %all-gather.5.cloned.1.call-done = bf16[768,7168]{1,0:T(8,128)(2,1)} async-done(((bf16[96,7168]{1,0:T(8,128)(2,1)}), bf16[768,7168]{1,0:T(8,128)(2,1)}) %all-gather.5.cloned.1.call-update) | async-done | bytes 11010064 | tf_op jit(solution)/shard_map/all_gather | solution.py:31
  325.1 17.8 %convolution_convert_fusion.2 = bf16[768,1024]{1,0:T(8,128)(2,1)} fusion(bf16[768,7168]{1,0:T(8,128)(2,1)} %all-gather.5.cloned.1.call-done, bf16[7168,1024]{1,0:T(8,128)(2,1)} %param.11), kind=kOutput, calls=%fused_computation.5 | convolution fusion | flops 11275075584 | bytes 27262976 | tf_op jit(solution)/shard_map/dot_general | solution.py:34
  342.9 0.0 reduce-scatter.5.cloned.1.call-update
  342.9 0.0 copy-done.2
  343.0 35.5 %reduce-scatter.5.cloned.1.call-done = bf16[192,1024]{1,0:T(8,128)(2,1)} async-done(((bf16[768,1024]{1,0:T(8,128)(2,1)}), bf16[192,1024]{1,0:T(8,128)(2,1)}) %reduce-scatter.5.cloned.1.call-update) | async-done | bytes 393232 | tf_op jit(solution)/shard_map/reduce_scatter | solution.py:33
  378.5 0.0 copy-done
  378.5 0.0 copy-done.1
  378.5 2.5 fusion.6
  381.0 39.2 %psum.15 = f32[]{:T(128)} all-reduce(f32[]{:T(128)} %get-tuple-element.2), channel_id=1, replica_groups=mesh['row'=8,'col'=4] {'row','col'}, use_global_device_ids=true, to_apply=%region_5.6 | all-reduce | flops 1 | bytes 8 | tf_op jit(solution)/shard_map/psum | solution.py:42
  (1 shorter events, 0.0 us)
Async XLA Ops:
  7.2 55.5 %all-gather.3.cloned.1.call-start = ((), (), s32[]{:S(2)}) async-start(), calls=%async_computation.2 | async-start | bytes 1966080 | tf_op jit(solution)/shard_map/all_gather | solution.py:20
  26.1 229.4 %reduce-scatter.3.cloned.1.call-start = ((), (), s32[]{:S(2)}) async-start(), calls=%async_computation.3 | async-start | bytes 24772608 | tf_op jit(solution)/shard_map/reduce_scatter | solution.py:25
  62.7 17.3 %copy-start.3 = (bf16[768,1024]{1,0:T(8,128)(2,1)S(1)}, bf16[768,1024]{1,0:T(8,128)(2,1)}, u32[]{:S(2)}) copy-start(bf16[768,1024]{1,0:T(8,128)(2,1)} %all-gather.3.cloned.1.call-done) | copy-start | bytes 4718596
  115.4 209.7 %all-gather.5.cloned.1.call-start = ((), (), s32[]{:S(2)}) async-start(), calls=%async_computation.4 | async-start | bytes 12386304 | tf_op jit(solution)/shard_map/all_gather | solution.py:31
  259.6 83.3 %copy-start.2 = (s32[2]{0:T(128)S(1)}, s32[2]{0:T(128)}, u32[]{:S(2)}) copy-start(s32[2]{0:T(128)} %param.13) | copy-start | bytes 28
  259.6 118.9 %copy-start = (bf16[192,1024]{1,0:T(8,128)(2,1)S(1)}, bf16[192,1024]{1,0:T(8,128)(2,1)}, u32[]{:S(2)}) copy-start(bf16[192,1024]{1,0:T(8,128)(2,1)} %param.7) | copy-start | bytes 1179652
  259.6 118.9 %copy-start.1 = (bf16[2,192,1024]{2,1,0:T(8,128)(2,1)S(1)}, bf16[2,192,1024]{2,1,0:T(8,128)(2,1)}, u32[]{:S(2)}) copy-start(bf16[2,192,1024]{2,1,0:T(8,128)(2,1)} %param.12) | copy-start | bytes 2359300
  259.6 118.8 %reduce-scatter.5.cloned.1.call-start = ((), (), s32[]{:S(2)}) async-start(), calls=%async_computation.5 | async-start | bytes 1966080 | tf_op jit(solution)/shard_map/reduce_scatter | solution.py:33
Sparse Core Ops, SparseCore 0:
  26.3 36.3 all-gather.2
  115.5 139.9 reduce-scatter.2
  259.7 65.3 all-gather.4
  343.0 35.4 reduce-scatter.4
where the time goes:
time: 429 us
  waiting for transfers between devices  277 us (65%)
  blocking collectives  54.4 us (13%)
  matrix products  54 us (13%)
  other arithmetic  26.8 us (6%)
  between operations  15.7 us (4%)
    reduce_scatter x1, waiting for transfers between devices, body(): lax.psum_scatter(jnp.concatenate([first, second], axis=1).astype(jnp.bflo...  140 us
    all_gather x1, waiting for transfers between devices, body(): hidden_all = lax.all_gather(swiglu(mine, width), 'row', axis=0, tiled=True)  65.2 us
    psum x1, blocking collectives, body(): total = lax.psum(jnp.sum(diff * diff), ('row', 'col'))  39.2 us
    all_gather x1, waiting for transfers between devices, body(): all_rows = lax.all_gather(normed, 'col', axis=0, tiled=True)  36.5 us
    reduce_scatter x1, waiting for transfers between devices, body(): lax.psum_scatter(jnp.dot(piece, w_down, preferred_element_type=jnp.float3...  35.5 us
    dot_general x1, matrix products, body(): first = jnp.dot(piece, w_gate, preferred_element_type=jnp.float32)  19 us
    dot_general x1, matrix products, body(): jnp.dot(piece, w_down, preferred_element_type=jnp.float32)  17.8 us
    dot_general x1, matrix products, body(): second = jnp.dot(piece, w_up, preferred_element_type=jnp.float32)  17.3 us
  transfers between devices with their start and end apart: 4, of which 4 were waited for; matrix products, arithmetic and copies ran while one was open for 0% of the time, Pallas kernels for 0%

commit v1 on v0

--- a/solution.py
+++ b/solution.py
@@ -17,7 +17,12 @@
     normed = (
         xf * lax.rsqrt(mean_sq[:, None] + 1e-05) * norm_gain.astype(jnp.float32)[None, :]
     ).astype(jnp.bfloat16)
-    all_rows = lax.all_gather(normed, "col", axis=0, tiled=True)
+    ring = [normed]
+    for hop in range(3):
+        ring.append(lax.ppermute(ring[-1], "col", [(dev, (dev + 1) % 4) for dev in range(4)]))
+    all_rows = jnp.roll(
+        jnp.concatenate(ring[::-1], axis=0), (lax.axis_index("col") + 1) * ring[0].shape[0], axis=0
+    )
     width = w_gate.shape[1]
     piece = all_rows
     first = jnp.dot(piece, w_gate, preferred_element_type=jnp.float32)

time: 429 us -> 429 us (level)
  local copies, waits for them, and re-layouts: 0.02 us -> 4.66 us
    all_gather x1 -> x0, waiting for transfers between devices: 36.5 us -> none  [body(): all_rows = lax.all_gather(normed, 'col', axis=0, tiled=True)]
    ppermute x0 -> x3, waiting for transfers between devices: none -> 28.9 us  [body(): lax.ppermute(ring[-1], 'col', [(dev, (dev + 1) % 4) for dev in range(4)])]
    unnamed x8 -> x12, local copies, waits for them, and re-layouts: 0.02 us -> 4.66 us
  transfers between devices with their start and end apart: 4 -> 6, of which waited for: 4 -> 6; matrix products, arithmetic and copies ran while one was open for 0% -> 0% of each run, Pallas kernels for 0% -> 0%
where the time goes in v1:
time: 429 us
  waiting for transfers between devices  274 us (64%)
  blocking collectives  54.4 us (13%)
  matrix products  50.7 us (12%)
  other arithmetic  27.7 us (6%)
  between operations  15.7 us (4%)
  local copies, waits for them, and re-layouts  4.66 us (1%)
    reduce_scatter x1, waiting for transfers between devices, body(): lax.psum_scatter(jnp.concatenate([first, second], axis=1).astype(jnp.bflo...  144 us
    all_gather x1, waiting for transfers between devices, body(): hidden_all = lax.all_gather(swiglu(mine, width), 'row', axis=0, tiled=True)  65.3 us
    psum x1, blocking collectives, body(): total = lax.psum(jnp.sum(diff * diff), ('row', 'col'))  39.2 us
    reduce_scatter x1, waiting for transfers between devices, body(): lax.psum_scatter(jnp.dot(piece, w_down, preferred_element_type=jnp.float3...  35.5 us
    ppermute x3, waiting for transfers between devices, body(): lax.ppermute(ring[-1], 'col', [(dev, (dev + 1) % 4) for dev in range(4)])  28.9 us
    dot_general x1, matrix products, body(): jnp.dot(piece, w_down, preferred_element_type=jnp.float32)  17.8 us
    dot_general x1, matrix products, body(): second = jnp.dot(piece, w_up, preferred_element_type=jnp.float32)  17.7 us
    concatenate x1, other arithmetic, body(): jnp.concatenate([first, second], axis=1).astype(jnp.bfloat16)  16.2 us
  transfers between devices with their start and end apart: 6, of which 6 were waited for; matrix products, arithmetic and copies ran while one was open for 0% of the time, Pallas kernels for 0%

profile of v1, /device:TPU:0, one launch (start us, length us, event | category | flops | bytes accessed | tf_op | source)
XLA Modules:
  0.0 428.7 jit_solution(9844173093033122962)
XLA Ops:
  7.2 0.0 reduce-scatter.3.cloned.1.call-start
  7.2 0.7 convert_element_type.35
  7.9 1.2 fusion.3
  9.1 15.1 %psum.14 = f32[192]{0:T(256)S(1)} all-reduce(f32[192]{0:T(256)S(1)} %fusion.3), channel_id=1, replica_groups=mesh['row'=8,'col'=4] {'row'}, use_global_device_ids=true, to_apply=%region_1.0 | all-reduce | flops 192 | bytes 1536 | tf_op jit(solution)/shard_map/psum | solution.py:15
  24.3 1.2 fusion.5
  25.4 1.6 collective-permute-start
  27.0 9.3 %collective-permute-done = bf16[192,1024]{1,0:T(8,128)(2,1)S(1)} collective-permute-done((bf16[192,1024]{1,0:T(8,128)(2,1)S(1)}, bf16[192,1024]{1,0:T(8,128)(2,1)S(1)}, u32[]{:S(2)}, u32[]{:S(2)}) %collective-permute-start) | collective-permute-done | bytes 393248 | tf_op jit(solution)/shard_map/ppermute | solution.py:22
  36.3 10.0 %collective-permute-done.1 = bf16[192,1024]{1,0:T(8,128)(2,1)S(1)} collective-permute-done((bf16[192,1024]{1,0:T(8,128)(2,1)S(1)}, bf16[192,1024]{1,0:T(8,128)(2,1)S(1)}, u32[]{:S(2)}, u32[]{:S(2)}) %collective-permute-start.1) | collective-permute-done | bytes 393248 | tf_op jit(solution)/shard_map/ppermute | solution.py:22
  46.4 9.6 %collective-permute-done.2 = bf16[192,1024]{1,0:T(8,128)(2,1)S(1)} collective-permute-done((bf16[192,1024]{1,0:T(8,128)(2,1)S(1)}, bf16[192,1024]{1,0:T(8,128)(2,1)S(1)}, u32[]{:S(2)}, u32[]{:S(2)}) %collective-permute-start.2) | collective-permute-done | bytes 393248 | tf_op jit(solution)/shard_map/ppermute | solution.py:22
  55.9 0.8 constant_dynamic-update-slice_fusion.7
  56.7 0.8 constant_dynamic-update-slice_fusion.6
  57.5 0.8 constant_dynamic-update-slice_fusion.5
  58.2 0.9 constant_dynamic-update-slice_fusion.4
  59.2 0.8 constant_dynamic-update-slice_fusion.3
  59.9 0.8 constant_dynamic-update-slice_fusion.2
  60.7 0.8 constant_dynamic-update-slice_fusion.1
  61.5 0.9 constant_dynamic-update-slice_fusion
  62.4 15.2 %convolution_convert_fusion.1 = bf16[768,7168]{1,0:T(8,128)(2,1)S(1)} fusion(bf16[1024,7168]{1,0:T(8,128)(2,1)} %param.9, bf16[1536,1024]{1,0:T(8,128)(2,1)} %constant_dynamic-update-slice_fusion, s32[]{:T(128)S(6)} %select_n.18), kind=kOutput, calls=%fused_computation.2 | convolution fusion | flops 11279794176 | bytes 27262980 | tf_op jit(solution)/shard_map/dot_general | solution.py:28
  77.7 17.7 %convolution_convert_fusion = bf16[768,7168]{1,0:T(8,128)(2,1)} fusion(bf16[1024,7168]{1,0:T(8,128)(2,1)} %param.10, bf16[1536,1024]{1,0:T(8,128)(2,1)} %constant_dynamic-update-slice_fusion, s32[]{:T(128)S(6)} %select_n.18), kind=kOutput, calls=%fused_computation.1 | convolution fusion | flops 11279794176 | bytes 27262980 | tf_op jit(solution)/shard_map/dot_general | solution.py:29
  95.3 16.2 %pad_maximum_fusion = bf16[768,14336]{1,0:T(8,128)(2,1)} fusion(bf16[768,7168]{1,0:T(8,128)(2,1)} %convolution_convert_fusion, bf16[768,7168]{1,0:T(8,128)(2,1)S(1)} %convolution_convert_fusion.1), kind=kLoop, calls=%fused_computation | loop fusion | flops 44040192 | bytes 44040192 | tf_op jit(solution)/shard_map/concatenate | solution.py:31
  111.5 0.0 reduce-scatter.3.cloned.1.call-update
  111.6 0.0 all-gather.2.cloned.1.call-start
  111.6 144.1 %reduce-scatter.3.cloned.1.call-done = bf16[96,14336]{1,0:T(8,128)(2,1)} async-done(((bf16[768,14336]{1,0:T(8,128)(2,1)}), bf16[96,14336]{1,0:T(8,128)(2,1)}) %reduce-scatter.3.cloned.1.call-update) | async-done | bytes 2752528 | tf_op jit(solution)/shard_map/reduce_scatter | solution.py:30
  255.7 2.3 convert_element_type.37
  258.0 1.8 fusion
  259.8 0.0 all-gather.2.cloned.1.call-update
  259.8 0.2 reduce-scatter.5.cloned.1.call-start
  260.0 65.3 %all-gather.2.cloned.1.call-done = bf16[768,7168]{1,0:T(8,128)(2,1)} async-done(((bf16[96,7168]{1,0:T(8,128)(2,1)}), bf16[768,7168]{1,0:T(8,128)(2,1)}) %all-gather.2.cloned.1.call-update) | async-done | bytes 11010064 | tf_op jit(solution)/shard_map/all_gather | solution.py:36
  325.3 17.8 %convolution_convert_fusion.2 = bf16[768,1024]{1,0:T(8,128)(2,1)} fusion(bf16[768,7168]{1,0:T(8,128)(2,1)} %all-gather.2.cloned.1.call-done, bf16[7168,1024]{1,0:T(8,128)(2,1)} %param.11), kind=kOutput, calls=%fused_computation.5 | convolution fusion | flops 11275075584 | bytes 27262976 | tf_op jit(solution)/shard_map/dot_general | solution.py:39
  343.2 35.5 %reduce-scatter.5.cloned.1.call-done = bf16[192,1024]{1,0:T(8,128)(2,1)} async-done(((bf16[768,1024]{1,0:T(8,128)(2,1)}), bf16[192,1024]{1,0:T(8,128)(2,1)}) %reduce-scatter.5.cloned.1.call-update) | async-done | bytes 393232 | tf_op jit(solution)/shard_map/reduce_scatter | solution.py:38
  378.7 2.5 fusion.8
  381.2 39.2 %psum.15 = f32[]{:T(128)} all-reduce(f32[]{:T(128)} %get-tuple-element.2), channel_id=1, replica_groups=mesh['row'=8,'col'=4] {'row','col'}, use_global_device_ids=true, to_apply=%region_5.6 | all-reduce | flops 1 | bytes 8 | tf_op jit(solution)/shard_map/psum | solution.py:47
  (10 shorter events, 0.0 us)
Async XLA Ops:
  7.2 51.1 %copy-start = (bf16[192,1024]{1,0:T(8,128)(2,1)S(1)}, bf16[192,1024]{1,0:T(8,128)(2,1)}, u32[]{:S(2)}) copy-start(bf16[192,1024]{1,0:T(8,128)(2,1)} %param.7) | copy-start | bytes 1179652
  7.2 248.5 %reduce-scatter.3.cloned.1.call-start = ((), (), s32[]{:S(2)}) async-start(), calls=%async_computation.2 | async-start | bytes 24772608 | tf_op jit(solution)/shard_map/reduce_scatter | solution.py:30
  25.4 10.9 %collective-permute-start = (bf16[192,1024]{1,0:T(8,128)(2,1)S(1)}, bf16[192,1024]{1,0:T(8,128)(2,1)S(1)}, u32[]{:S(2)}, u32[]{:S(2)}) collective-permute-start(bf16[192,1024]{1,0:T(8,128)(2,1)S(1)} %fusion.5), channel_id=1, source_target_pairs={{0,1},{1,2},{2,3},{3,0},{4,5},{5,6},{6,7},{7,4},{8,9},{9,10},{10,1... | collective-permute-start | bytes 1179656 | tf_op jit(solution)/shard_map/ppermute | solution.py:22
  36.3 10.0 %collective-permute-start.1 = (bf16[192,1024]{1,0:T(8,128)(2,1)S(1)}, bf16[192,1024]{1,0:T(8,128)(2,1)S(1)}, u32[]{:S(2)}, u32[]{:S(2)}) collective-permute-start(bf16[192,1024]{1,0:T(8,128)(2,1)S(1)} %collective-permute-done), channel_id=1, source_target_pairs={{0,1},{1,2},{2,3},{3,0},{4,5},{5,6},{6,7},{7,4},{8,9},{9,10},{10,1... | collective-permute-start | bytes 1179656 | tf_op jit(solution)/shard_map/ppermute | solution.py:22
  46.3 9.6 %collective-permute-start.2 = (bf16[192,1024]{1,0:T(8,128)(2,1)S(1)}, bf16[192,1024]{1,0:T(8,128)(2,1)S(1)}, u32[]{:S(2)}, u32[]{:S(2)}) collective-permute-start(bf16[192,1024]{1,0:T(8,128)(2,1)S(1)} %collective-permute-done.1), channel_id=1, source_target_pairs={{0,1},{1,2},{2,3},{3,0},{4,5},{5,6},{6,7},{7,4},{8,9},{9,10},{10,1... | collective-permute-start | bytes 1179656 | tf_op jit(solution)/shard_map/ppermute | solution.py:22
  111.6 213.7 %all-gather.2.cloned.1.call-start = ((), (), s32[]{:S(2)}) async-start(), calls=%async_computation.3 | async-start | bytes 12386304 | tf_op jit(solution)/shard_map/all_gather | solution.py:36
  259.8 83.3 %copy-start.2 = (s32[2]{0:T(128)S(1)}, s32[2]{0:T(128)}, u32[]{:S(2)}) copy-start(s32[2]{0:T(128)} %param.13) | copy-start | bytes 28
  259.8 118.9 %copy-start.1 = (bf16[2,192,1024]{2,1,0:T(8,128)(2,1)S(1)}, bf16[2,192,1024]{2,1,0:T(8,128)(2,1)}, u32[]{:S(2)}) copy-start(bf16[2,192,1024]{2,1,0:T(8,128)(2,1)} %param.12) | copy-start | bytes 2359300
  259.8 118.9 %reduce-scatter.5.cloned.1.call-start = ((), (), s32[]{:S(2)}) async-start(), calls=%async_computation.4 | async-start | bytes 1966080 | tf_op jit(solution)/shard_map/reduce_scatter | solution.py:38
Sparse Core Ops, SparseCore 0:
  111.7 143.9 reduce-scatter.2
  259.9 65.3 all-gather.1
  343.2 35.4 reduce-scatter.4
